TPU v7x, 128 devices: a whole 4x4x4 slice. The times are simulated.
128 devices in a mesh: pb: 16 (over z, x_lo, core), pa: 8 (over y, x_hi).
Axes of the slice: x: 4 (x_hi: 2, x_lo: 2; x = x_hi * 2 + x_lo), y: 4, z: 4, core: 2. Of those that a mesh axis runs over, the one named last changes fastest.
Arguments:
- queries: float32 [16384, 1024], P('pb'), may hold values from -64 to 64
- passages: float32 [16384, 1024], P(('pb', 'pa')), may hold values from -64 to 64
- hard_ids: int32 [16384, 7], P('pb'), may hold values from 0 to 16383
Outputs:
- loss: float32 [], replicated
- query_grads: float32 [16384, 1024], P(('pb', 'pa'))
- passage_grads: float32 [16384, 1024], P(('pb', 'pa'))
All inputs are finite; a program needn't handle non-finite values.
Results may differ from a plain program's by a relative error of at most 0.0003.
Values sent between devices are 32-bit elements; how exact they have to be, the bound alone decides.
No kernel may reach another device: no remote copies, remote signals or barrier semaphores. Data moves between devices by JAX's collectives and lax.ppermute only.
A program may use at most 128 MiB of HBM per device.

v0:
```python
import math

import jax
import jax.numpy as jnp
from jax import lax
from jax.sharding import PartitionSpec as P

HARD = 7


def precise_dot(left, right):
    return jnp.dot(left, right, precision=lax.Precision.HIGHEST, preferred_element_type=jnp.float32)


def on_device(queries, passages, hard_ids):
    query_count, width = queries.shape
    passage_count = passages.shape[0]
    n_block = lax.axis_size("pb")
    n_column = lax.axis_size("pa")
    column = lax.axis_index("pa")
    query_block = lax.axis_index("pb")
    scale = 1.0 / math.sqrt(width)
    total_cols = n_block * passage_count
    row_index = jnp.arange(total_cols, dtype=jnp.int32)
    column_ids = (
        row_index // passage_count * n_column + column
    ) * passage_count + row_index % passage_count
    query_ids = query_block * query_count + jnp.arange(query_count, dtype=jnp.int32)
    counts = jnp.ones((query_count, total_cols), jnp.float32)
    for k in range(HARD):
        counts = counts + (hard_ids[:, k : k + 1] == column_ids[None, :]).astype(jnp.float32)
    gathered = lax.all_gather(passages, "pb", axis=0, tiled=True)
    logits = precise_dot(queries, gathered.T) * scale
    local_max = jnp.max(logits, axis=1)
    local_total = jnp.sum(counts * jnp.exp(logits - local_max[:, None]), axis=1)
    row_max = lax.pmax(local_max, "pa")
    row_total = lax.psum(local_total * jnp.exp(local_max - row_max), "pa")
    lse = row_max + jnp.log(row_total)
    positive = column_ids[None, :] == query_ids[:, None]
    has_positive = jnp.any(positive, axis=1)
    pos_logit = jnp.sum(jnp.where(positive, logits, 0.0), axis=1)
    loss_local = jnp.sum(jnp.where(has_positive, lse - pos_logit, 0.0))
    loss = lax.psum(loss_local, ("pb", "pa")) / (query_count * n_block)
    coeff = counts * jnp.exp(logits - lse[:, None]) - positive.astype(jnp.float32)
    query_part = precise_dot(coeff, gathered) * scale
    query_grads = lax.psum_scatter(query_part, "pa", scatter_dimension=0, tiled=True)
    product = lax.dot_general(
        coeff,
        queries,
        (((0,), (0,)), ((), ())),
        precision=lax.Precision.HIGHEST,
        preferred_element_type=jnp.float32,
    )
    passage_grads = lax.psum_scatter(product * scale, "pb", scatter_dimension=0, tiled=True)
    return (loss, query_grads, passage_grads)


def solution(mesh):
    placed = (P("pb", None), P(("pb", "pa"), None), P("pb", None))
    return jax.shard_map(
        on_device,
        mesh=mesh,
        in_specs=placed,
        out_specs=(P(), P(("pb", "pa"), None), P(("pb", "pa"), None)),
        check_vma=False,
    )
```

profile of v0, /device:TPU:0, one launch (start us, length us, event | category | flops | bytes accessed | tf_op | source)
XLA Modules:
  0.0 390.9 jit_solution(8196182338651346863)
XLA Ops:
  7.2 0.0 all-gather.2.cloned.1.call-start
  7.2 0.7 all-gather.2.cloned.1.call-update
  7.9 0.0 reduce-scatter.3.cloned.1.call-start
  8.0 1.2 compare_reduce_fusion
  9.1 1.1 fusion.13
  10.2 54.1 %all-gather.2.cloned.1.call-done = f32[2048,1024]{1,0:T(8,128)} async-done(((f32[128,1024]{1,0:T(8,128)}), f32[2048,1024]{1,0:T(8,128)}) %all-gather.2.cloned.1.call-update) | async-done | bytes 8388624 | tf_op jit(solution)/shard_map/all_gather | solution.py:32
  64.3 31.2 %multiply_reduce_fusion.1 = (f32[1024]{0:T(1024)S(1)}, f32[1024,2048]{1,0:T(8,128)}) fusion(f32[1024,1024]{1,0:T(8,128)} %param.3, f32[2048,1024]{1,0:T(8,128)} %all-gather.2.cloned.1.call-done), kind=kOutput, calls=%fused_computation.7 | convolution fusion | flops 25773998080 | bytes 20975616 | tf_op jit(solution)/shard_map/dot_general | solution.py:12
  95.5 24.2 %pmax.7 = f32[1024]{0:T(1024)S(1)} all-reduce(f32[1024]{0:T(1024)S(1)} %get-tuple-element.14), channel_id=1, replica_groups=mesh['pb'=16,'pa'=8] {'pa'}, use_global_device_ids=true, to_apply=%region_2.3 | all-reduce | flops 1024 | bytes 8192 | tf_op jit(solution)/shard_map/pmax | solution.py:36
  119.7 10.9 %fusion = (f32[1024]{0:T(1024)S(1)}, f32[1024]{0:T(1024)S(1)}) fusion(f32[1024,2048]{1,0:T(8,128)} %get-tuple-element.15, s32[2048]{0:T(1024)S(1)} %fusion.11, s32[1024]{0:T(1024)S(1)} %iota_add_fusion, f32[1024]{0:T(1024)S(1)} %get-tuple-element.14, s32[1024]{0:T(1024)S(1)} %bitcast.23, s32[1024]{0:T(1024)S(1)} %bitcast.25, s32[1024]{0:T(1024)S(1)} %bitcast.15, ...), kind=kLoop, calls=%fused_computation.3 | loop fusion | flops 58718208 | bytes 8441856 | tf_op jit(solution)/shard_map/reduce_sum | solution.py:41
  130.6 19.1 %psum.14 = f32[1024]{0:T(1024)S(1)} all-reduce(f32[1024]{0:T(1024)S(1)} %exponential_multiply_fusion), channel_id=1, replica_groups=mesh['pb'=16,'pa'=8] {'pa'}, use_global_device_ids=true, to_apply=%region_4.5 | all-reduce | flops 1024 | bytes 8192 | tf_op jit(solution)/shard_map/psum | solution.py:37
  149.7 0.6 select_reduce_fusion
  150.3 10.5 %fusion.1 = f32[1024,2048]{1,0:T(8,128)S(1)} fusion(f32[1024,2048]{1,0:T(8,128)} %get-tuple-element.15, f32[1024]{0:T(1024)S(1)} %get-tuple-element.6, s32[2048]{0:T(1024)S(1)} %fusion.11, s32[1024]{0:T(1024)S(1)} %bitcast.24, s32[1024]{0:T(1024)S(1)} %bitcast.26, s32[1024]{0:T(1024)S(1)} %bitcast.16, s32[1024]{0:T(1024)S(1)} %bitcast.18, ...), kind=kLoop, calls=%fused_computation.4 | loop fusion | flops 56623104 | bytes 16822272 | tf_op jit(solution)/shard_map/sub | solution.py:44
  160.8 0.0 copy-start
  160.8 3.2 copy-done
  164.0 34.9 %convolution_multiply_fusion.1 = f32[1024,1024]{1,0:T(8,128)} fusion(f32[1024,2048]{1,0:T(8,128)S(1)} %fusion.1, f32[2048,1024]{1,0:T(8,128)} %all-gather.2.cloned.1.call-done), kind=kOutput, calls=%fused_computation.9 | convolution fusion | flops 25770852352 | bytes 20971520 | tf_op jit(solution)/shard_map/dot_general | solution.py:12
  198.9 0.0 reduce-scatter.3.cloned.1.call-update
  198.9 0.2 reduce-scatter.5.cloned.1.call-start
  199.2 31.2 %convolution_multiply_fusion = f32[2048,1024]{1,0:T(8,128)} fusion(f32[1024,2048]{1,0:T(8,128)} %copy-done, f32[1024,1024]{1,0:T(8,128)} %param.3), kind=kOutput, calls=%fused_computation.8 | convolution fusion | flops 25771900928 | bytes 20971520 | tf_op jit(solution)/shard_map/dot_general | solution.py:47
  230.4 0.0 reduce-scatter.5.cloned.1.call-update
  230.4 67.5 %psum.15 = f32[]{:T(128)} all-reduce(f32[]{:T(128)} %get-tuple-element.5), channel_id=1, replica_groups=mesh['pb'=16,'pa'=8] {'pb','pa'}, use_global_device_ids=true, to_apply=%region_7.8 | all-reduce | flops 1 | bytes 8 | tf_op jit(solution)/shard_map/psum | solution.py:43
  298.5 0.0 reduce-scatter.3.cloned.1.call-done
  298.6 84.7 %reduce-scatter.5.cloned.1.call-done = f32[128,1024]{1,0:T(8,128)} async-done(((f32[2048,1024]{1,0:T(8,128)}), f32[128,1024]{1,0:T(8,128)}) %reduce-scatter.5.cloned.1.call-update) | async-done | bytes 524304 | tf_op jit(solution)/shard_map/reduce_scatter | solution.py:54
  (3 shorter events, 0.0 us)
Async XLA Ops:
  7.2 57.1 %all-gather.2.cloned.1.call-start = ((), (), s32[]{:S(2)}) async-start(), calls=%async_computation.2 | async-start | bytes 8912896 | tf_op jit(solution)/shard_map/all_gather | solution.py:32
  7.9 290.7 %reduce-scatter.3.cloned.1.call-start = ((), (), s32[]{:S(2)}) async-start(), calls=%async_computation.3 | async-start | bytes 4718592 | tf_op jit(solution)/shard_map/reduce_scatter | solution.py:46
  160.8 3.2 copy-start
  198.9 184.3 %reduce-scatter.5.cloned.1.call-start = ((), (), s32[]{:S(2)}) async-start(), calls=%async_computation.4 | async-start | bytes 8912896 | tf_op jit(solution)/shard_map/reduce_scatter | solution.py:54
Sparse Core Ops, SparseCore 0:
  9.7 54.5 all-gather.1
  199.0 84.3 reduce-scatter.2
  286.5 96.7 reduce-scatter.4
where the time goes:
time: 392 us; the launch traced here: 391 us
  waiting for transfers between devices  140 us (36%)
  blocking collectives  111 us (28%)
  matrix products  97.3 us (25%)
  other arithmetic  23.2 us (6%)
  between operations  15.6 us (4%)
  local copies, waits for them, and re-layouts  4.25 us (1%)
    reduce_scatter x1, waiting for transfers between devices, on_device(): lax.psum_scatter(product * scale, 'pb', scatter_dimension=0, tiled=True)  84.7 us
    psum x1, blocking collectives, on_device(): loss = lax.psum(loss_local, ('pb', 'pa')) / (query_count * n_block)  67.5 us
    dot_general x2, matrix products, precise_dot(): jnp.dot(left, right, precision=lax.Precision.HIGHEST, preferred_element_t...  66.1 us
    all_gather x1, waiting for transfers between devices, on_device(): gathered = lax.all_gather(passages, 'pb', axis=0, tiled=True)  54.1 us
    dot_general x1, matrix products, on_device(): lax.dot_general(coeff, queries, (((0,), (0,)), ((), ())), precision=lax.P...  31.2 us
    pmax x1, blocking collectives, on_device(): row_max = lax.pmax(local_max, 'pa')  24.2 us
    psum x1, blocking collectives, on_device(): row_total = lax.psum(local_total * jnp.exp(local_max - row_max), 'pa')  19.1 us
    reduce_sum x1, other arithmetic, on_device(): pos_logit = jnp.sum(jnp.where(positive, logits, 0.0), axis=1)  10.9 us
  transfers between devices with their start and end apart: 3, of which 2 were waited for; matrix products, arithmetic and copies ran while one was open for 9% of the time, Pallas kernels for 0%

commit v1 on v0

v1 whole, which is shorter than its diff:
```python
import functools
import math

import jax
import jax.numpy as jnp
from jax import lax
from jax.experimental import pallas as pl
from jax.experimental.pallas import tpu as pltpu
from jax.sharding import PartitionSpec as P

HARD = 7
AXES = ("pb", "pa")
N_PB, N_PA = 16, 8
INTERPRET = False
F32, BF16 = jnp.float32, jnp.bfloat16
MIB = 1 << 20


def route(z=0, xl=0, core=0, y=0, xh=0, yxor=0, zxor=0):
    pairs = []
    for device in range(N_PB * N_PA):
        pb, pa = divmod(device, N_PA)
        to_z = ((pb // 4 + z) % 4) ^ zxor
        to_y = ((pa // 2 + y) % 4) ^ yxor
        to_pb = to_z * 4 + ((pb // 2 % 2) ^ xl) * 2 + (pb % 2 ^ core)
        pairs.append((device, to_pb * N_PA + to_y * 2 + (pa % 2 ^ xh)))
    return pairs


def send(x, **to):
    return lax.ppermute(x, AXES, route(**to))


def params(limit=40):
    return pltpu.CompilerParams(vmem_limit_bytes=limit * MIB)


def halves(x):
    hi = x.astype(BF16)
    return hi, (x - hi.astype(F32)).astype(BF16)


def split_kernel(a_ref, b_ref, hi_ref, lo_ref):
    own = pl.program_id(0) < pl.num_programs(0) // 2

    def put(ref):
        hi_ref[...], lo_ref[...] = halves(ref[...])

    pl.when(own)(lambda: put(a_ref))
    pl.when(jnp.logical_not(own))(lambda: put(b_ref))


def split_rows(a, b):
    rows, width = a.shape
    tile = min(256, rows)
    steps = rows // tile
    out = jax.ShapeDtypeStruct((2 * rows, width), BF16)
    return pl.pallas_call(
        split_kernel,
        out_shape=(out, out),
        grid=(2 * steps,),
        in_specs=[
            pl.BlockSpec((tile, width), lambda t: (jnp.minimum(t, steps - 1), 0)),
            pl.BlockSpec((tile, width), lambda t: (jnp.maximum(t - steps, 0), 0)),
        ],
        out_specs=[pl.BlockSpec((tile, width), lambda t: (t, 0))] * 2,
        compiler_params=params(),
        cost_estimate=pl.CostEstimate(flops=4 * rows * width, bytes_accessed=16 * rows * width, transcendentals=0),
        interpret=INTERPRET,
        name="split_rows",
    )(a, b)


NT = (((1,), (1,)), ((), ()))
TN = (((0,), (0,)), ((), ()))


def dot(a, b, dims):
    return lax.dot_general(a, b, dims, preferred_element_type=F32)


def score_kernel(rows, first, scale, base_ref, *refs):
    count = len(rows)
    blocks = refs[:count]
    qh_ref, ql_ref, ids_ref = refs[count : count + 3]
    refs = refs[count + 3 :]
    prev_ref = None
    if not first:
        prev_ref, refs = refs[0], refs[1:]
    e_ref, stat_ref, hi_ref, lo_ref, both = refs
    total = sum(rows)
    step = pl.program_id(0)
    tile = qh_ref.shape[0]

    @pl.when(step == 0)
    def _():
        at = 0
        for block, n in zip(blocks, rows):
            hi, lo = halves(block[...])
            both[at : at + n, :] = hi
            both[total + at : total + at + n, :] = lo
            hi_ref[at : at + n, :] = hi
            lo_ref[at : at + n, :] = lo
            at += n

    x = dot(both[...], qh_ref[...], NT)
    y = dot(both[:total, :], ql_ref[...], NT)
    s = (x[:total] + x[total:] + y) * scale
    top = jnp.max(s, axis=0, keepdims=True)
    if first:
        high = top
    else:
        before = prev_ref[0:1, :]
        high = jnp.maximum(before, top)
    e = jnp.exp(s - high)
    ids = ids_ref[...]
    parts = []
    at = 0
    for index, n in enumerate(rows):
        near = ids - base_ref[index]
        row = lax.broadcasted_iota(jnp.int32, (n, tile), 0)
        c = jnp.ones((n, tile), F32)
        for k in range(HARD):
            c = c + jnp.where(row == near[k : k + 1, :], 1.0, 0.0)
        parts.append(c * e[at : at + n])
        at += n
    ce = parts[0] if count == 1 else jnp.concatenate(parts, axis=0)
    mass = jnp.sum(ce, axis=0, keepdims=True)
    if first:
        lane = lax.broadcasted_iota(jnp.int32, (total, tile), 1) + step * tile - base_ref[count]
        positive = lax.broadcasted_iota(jnp.int32, (total, tile), 0) == lane
        pos = jnp.sum(jnp.where(positive, s, 0.0), axis=0, keepdims=True)
        ce = jnp.where(positive, 0.0, ce)
    else:
        pos = prev_ref[2:3, :]
        mass = mass + prev_ref[1:2, :] * jnp.exp(before - high)
    e_ref[...] = ce
    stat_ref[...] = jnp.concatenate([high, mass, pos, jnp.zeros((5, tile), F32)], axis=0)


def score(blocks, bases, qh, ql, ids, prev, scale):
    rows = tuple(b.shape[0] for b in blocks)
    total = sum(rows)
    queries, width = qh.shape
    tile = min(256, queries)
    whole = [pl.BlockSpec((n, width), lambda t, s: (0, 0)) for n in rows]
    args = list(blocks) + [qh, ql, ids]
    specs = whole + [
        pl.BlockSpec((tile, width), lambda t, s: (t, 0)),
        pl.BlockSpec((tile, width), lambda t, s: (t, 0)),
        pl.BlockSpec((8, tile), lambda t, s: (0, t)),
    ]
    if prev is not None:
        args.append(prev)
        specs.append(pl.BlockSpec((8, tile), lambda t, s: (0, t)))
    return pl.pallas_call(
        functools.partial(score_kernel, rows, prev is None, scale),
        out_shape=(
            jax.ShapeDtypeStruct((total, queries), F32),
            jax.ShapeDtypeStruct((8, queries), F32),
            jax.ShapeDtypeStruct((total, width), BF16),
            jax.ShapeDtypeStruct((total, width), BF16),
        ),
        grid_spec=pltpu.PrefetchScalarGridSpec(
            num_scalar_prefetch=1,
            grid=(queries // tile,),
            in_specs=specs,
            out_specs=[
                pl.BlockSpec((total, tile), lambda t, s: (0, t)),
                pl.BlockSpec((8, tile), lambda t, s: (0, t)),
                pl.BlockSpec((total, width), lambda t, s: (0, 0)),
                pl.BlockSpec((total, width), lambda t, s: (0, 0)),
            ],
            scratch_shapes=[pltpu.VMEM((2 * total, width), BF16)],
        ),
        compiler_params=params(),
        cost_estimate=pl.CostEstimate(
            flops=6 * total * queries * width, bytes_accessed=4 * (total * width + queries * width + total * queries), transcendentals=total * queries
        ),
        interpret=INTERPRET,
        name=f"score_{total}",
    )(bases, *args)


def query_kernel(groups, *refs):
    e_refs, stat_refs = refs[:groups], refs[groups : 2 * groups]
    hi_refs, lo_refs = refs[2 * groups : 3 * groups], refs[3 * groups : 4 * groups]
    out_ref = refs[4 * groups]
    last = stat_refs[-1][0:1, :]
    acc = None
    for g in range(groups):
        a = e_refs[g][...]
        if g < groups - 1:
            a = a * jnp.exp(stat_refs[g][0:1, :] - last)
        hi, lo = halves(a)
        ph, pw = hi_refs[g][...], lo_refs[g][...]
        part = dot(hi, ph, TN) + dot(lo, ph, TN) + dot(hi, pw, TN)
        acc = part if acc is None else acc + part
    out_ref[...] = acc


def query_part(es, stats, his, los, first_row, n_rows):
    width = his[0].shape[1]
    tile = min(256, n_rows)
    start = first_row // tile
    groups = len(es)
    depth = sum(e.shape[0] for e in es)
    specs = [pl.BlockSpec((e.shape[0], tile), lambda t: (0, t + start)) for e in es]
    specs += [pl.BlockSpec((8, tile), lambda t: (0, t + start))] * groups
    specs += [pl.BlockSpec(h.shape, lambda t: (0, 0)) for h in his] * 2
    return pl.pallas_call(
        functools.partial(query_kernel, groups),
        out_shape=jax.ShapeDtypeStruct((n_rows, width), F32),
        grid=(n_rows // tile,),
        in_specs=specs,
        out_specs=pl.BlockSpec((tile, width), lambda t: (t, 0)),
        compiler_params=params(),
        cost_estimate=pl.CostEstimate(
            flops=6 * depth * n_rows * width, bytes_accessed=4 * (depth * width + n_rows * width + depth * n_rows), transcendentals=0
        ),
        interpret=INTERPRET,
        name="query_part",
    )(*es, *stats, *his, *los)


def passage_kernel(rows, scale, e_ref, stat_ref, lse_ref, qh_ref, ql_ref, *refs):
    outs, both = refs[:-1], refs[-1]
    total = sum(rows)

    @pl.when(pl.program_id(0) == 0)
    def _():
        a = e_ref[...] * (jnp.exp(stat_ref[0:1, :] - lse_ref[0:1, :]) * scale)
        hi, lo = halves(a)
        both[:total, :] = hi
        both[total:, :] = lo

    x = jnp.dot(both[...], qh_ref[...], preferred_element_type=F32)
    y = jnp.dot(both[:total, :], ql_ref[...], preferred_element_type=F32)
    r = x[:total] + x[total:] + y
    at = 0
    for out, n in zip(outs, rows):
        out[...] = r[at : at + n]
        at += n


def passage_part(e, stat, lse, qh, ql, rows, scale):
    total, queries = e.shape
    width = qh.shape[1]
    tile = min(256, width)
    return pl.pallas_call(
        functools.partial(passage_kernel, tuple(rows), scale),
        out_shape=tuple(jax.ShapeDtypeStruct((n, width), F32) for n in rows),
        grid=(width // tile,),
        in_specs=[
            pl.BlockSpec((total, queries), lambda t: (0, 0)),
            pl.BlockSpec((8, queries), lambda t: (0, 0)),
            pl.BlockSpec((8, queries), lambda t: (0, 0)),
            pl.BlockSpec((queries, tile), lambda t: (0, t)),
            pl.BlockSpec((queries, tile), lambda t: (0, t)),
        ],
        out_specs=[pl.BlockSpec((n, tile), lambda t: (0, t)) for n in rows],
        scratch_shapes=[pltpu.VMEM((2 * total, queries), BF16)],
        compiler_params=params(),
        cost_estimate=pl.CostEstimate(
            flops=6 * total * queries * width, bytes_accessed=4 * (total * width + queries * width + total * queries), transcendentals=0
        ),
        interpret=INTERPRET,
        name=f"passage_part_{total}",
    )(e, stat, lse, qh, ql)


def merge(a, b):
    keep = a[0] >= b[0]
    small, big = jnp.where(keep, b[1], a[1]), jnp.where(keep, a[1], b[1])
    total = big + small * jnp.exp(-jnp.abs(a[0] - b[0]))
    return jnp.stack([jnp.maximum(a[0], b[0]), total, a[2] + b[2]])


def scatter_sum(blocks, plus, minus, swap):
    half = blocks[0][0].shape[0] // 2
    sums = []
    for dx in (1, 0):
        near, right, far, left = blocks[dx][0], blocks[dx][1], blocks[dx][2], blocks[dx][3]
        from_left = plus(far[:half])
        from_right = minus(far[half:])
        right = jnp.concatenate([right[:half] + from_left, right[half:]], axis=0)
        left = jnp.concatenate([left[:half], left[half:] + from_right], axis=0)
        near = near + plus(right) + minus(left)
        sums.append(swap(near) if dx == 1 else near)
    return sums[0] + sums[1]


def on_device(queries, passages, hard_ids):
    block, width = queries.shape
    shard = passages.shape[0]
    half = shard // 2
    scale = 1.0 / math.sqrt(width)
    pb, pa = lax.axis_index("pb"), lax.axis_index("pa")
    z, xl, core = pb // 4, pb // 2 % 2, pb % 2
    y, xh = pa // 2, pa % 2

    ids = jnp.concatenate([hard_ids.T, jnp.full((8 - HARD, block), -1, jnp.int32)], axis=0)
    across = send(passages, xl=1)
    down = send(passages, z=1)
    up = send(passages, z=-1)
    partner = send(queries, core=1)
    ids = jnp.concatenate([ids, send(ids, core=1)], axis=1)
    qh, ql = split_rows(queries, partner)

    def base(dz, dx, offset=0):
        owner = ((z + dz) % 4) * 4 + (xl ^ dx) * 2 + core
        return (owner * N_PA + pa) * shard + offset

    def bases(*entries):
        return jnp.stack(entries).astype(jnp.int32)

    groups = []
    prev = None

    def run(blocks, at):
        nonlocal prev
        e, prev, hi, lo = score(blocks, at, qh, ql, ids, prev, scale)
        groups.append((e, prev, hi, lo))

    run([passages], bases(base(0, 0), pa * shard))
    down_x = send(across, z=1)
    up_x = send(across, z=-1)
    far_a = send(down[:half], z=1)
    far_b = send(up[half:], z=-1)
    run([across, down, up], bases(base(0, 1), base(3, 0), base(1, 0)))
    far_xa = send(down_x[:half], z=1)
    far_xb = send(up_x[half:], z=-1)
    run([down_x, up_x, far_a, far_b], bases(base(3, 1), base(1, 1), base(2, 0), base(2, 0, half)))
    run([far_xa, far_xb], bases(base(2, 1), base(2, 1, half)))

    es, stats, his, los = (list(t) for t in zip(*groups))

    mine = prev[:3]
    other = send(mine, core=1)
    other = jnp.concatenate([other[:, block:], other[:, :block]], axis=1)
    rec = merge(mine, other)
    for to in (dict(yxor=1), dict(yxor=2), dict(xh=1)):
        rec = merge(rec, send(rec, **to))

    quarter = block // 2
    theirs = [query_part(es, stats, his, los, block + r, quarter) for r in (0, quarter)]
    ours = [query_part(es, stats, his, los, r, quarter) for r in (0, quarter)]
    from_partner = [send(t, core=1) for t in theirs]

    lse = rec[0] + jnp.log(rec[1])
    lse8 = jnp.broadcast_to(lse[None, :], (8, 2 * block))

    (g21,) = passage_part(es[3], stats[3], lse8, qh, ql, (shard,), scale)
    g31, g11, g20 = passage_part(es[2], stats[2], lse8, qh, ql, (shard,) * 3, scale)
    g01, g30, g10 = passage_part(es[1], stats[1], lse8, qh, ql, (shard,) * 3, scale)
    (g00,) = passage_part(es[0], stats[0], lse8, qh, ql, (shard,), scale)
    passage_sum = scatter_sum(
        [[g00, g10, g20, g30], [g01, g11, g21, g31]],
        lambda v: send(v, z=1),
        lambda v: send(v, z=-1),
        lambda v: send(v, xl=1),
    )

    ours, from_partner = jnp.concatenate(ours, 0), jnp.concatenate(from_partner, 0)
    own_scale = (jnp.exp(mine[0, :block] - lse[:block]) * scale)[:, None]
    other_scale = (jnp.exp(other[0, :block] - lse[:block]) * scale)[:, None]

    def rows_for(dy, dx):
        at = (((y + dy) % 4) * 2 + (xh ^ dx)) * shard

        def cut(v):
            return lax.dynamic_slice_in_dim(v, at, shard, 0)

        return cut(ours) * cut(own_scale) + cut(from_partner) * cut(other_scale)

    query_sum = scatter_sum(
        [[rows_for(dy, dx) for dy in range(4)] for dx in range(2)],
        lambda v: send(v, y=1),
        lambda v: send(v, y=-1),
        lambda v: send(v, xh=1),
    )

    def own(v):
        return lax.dynamic_slice_in_dim(v, pa * shard, shard, 0)

    row_ids = pb * block + pa * shard + jnp.arange(shard, dtype=jnp.int32)
    own_ids = lax.dynamic_slice_in_dim(ids, pa * shard, shard, 1)
    tally = 1.0 + jnp.sum((own_ids == row_ids[None, :]).astype(F32), axis=0)
    coeff = (tally * jnp.exp(own(rec[2]) - own(lse)) - 1.0) * scale
    query_grads = query_sum + coeff[:, None] * passages
    passage_grads = passage_sum + coeff[:, None] * own(queries)

    sums = jnp.sum((lse - rec[2]).reshape(2, block), axis=1)
    loss = jnp.broadcast_to(sums[0] + sums[1], (8, 128))
    for to in (dict(zxor=1), dict(zxor=2), dict(xl=1)):
        loss = loss + send(loss, **to)
    loss = loss[0, 0] / (block * N_PB)
    return loss, query_grads, passage_grads


def solution(mesh):
    placed = (P("pb", None), P(("pb", "pa"), None), P("pb", None))
    return jax.shard_map(
        on_device,
        mesh=mesh,
        in_specs=placed,
        out_specs=(P(), P(("pb", "pa"), None), P(("pb", "pa"), None)),
        check_vma=False,
    )
```

time: 392 us -> 249 us (0.64)
  blocking collectives: 111 us -> 0 us
  waiting for transfers between devices: 140 us -> 41.4 us
  matrix products: 97.3 us -> 0 us
  Pallas kernels: 0 us -> 94.8 us
  starting transfers between devices: 0.3 us -> 51.8 us
  local copies, waits for them, and re-layouts: 4.25 us -> 40.4 us
  between operations: 15.6 us -> 4.65 us
  other arithmetic: 23.2 us -> 14.7 us
    dot_general x3 -> x0, matrix products: 97.3 us -> none  [the longest x2 66.1 us: precise_dot(): jnp.dot(left, right, precision=lax.Precision.HIGHEST, preferred_element_t...]
    pallas_call x0 -> x13, Pallas kernels: none -> 94.8 us  [the longest x4 40.6 us: score(): pl.pallas_call(functools.partial(score_kernel, rows, prev is None, scale)...]
    psum x2 -> x0, blocking collectives: 86.5 us -> none  [the longest x1 67.5 us: on_device(): loss = lax.psum(loss_local, ('pb', 'pa')) / (query_count * n_block)]
    reduce_scatter x2 -> x0, waiting for transfers between devices: 84.7 us -> none  [the longest x1 84.7 us: on_device(): lax.psum_scatter(product * scale, 'pb', scatter_dimension=0, tiled=True)]
    all_gather x1 -> x0, waiting for transfers between devices: 54.1 us -> none  [on_device(): gathered = lax.all_gather(passages, 'pb', axis=0, tiled=True)]
    ppermute x0 -> x38, starting transfers between devices: none -> 51.8 us  [send(): return lax.ppermute(x, AXES, route(**to))]
    ppermute x0 -> x38, waiting for transfers between devices: none -> 41.4 us  [send(): return lax.ppermute(x, AXES, route(**to))]
    unnamed x2 -> x87, local copies, waits for them, and re-layouts: 3.2 us -> 31.8 us
  transfers between devices with their start and end apart: 3 -> 38, of which waited for: 2 -> 9; matrix products, arithmetic and copies ran while one was open for 9% -> 9% of each run, Pallas kernels for 0% -> 36%
where the time goes in v1:
time: 249 us; the launch traced here: 248 us
  Pallas kernels  94.8 us (38%)
  starting transfers between devices  51.8 us (21%)
  waiting for transfers between devices  41.4 us (17%)
  local copies, waits for them, and re-layouts  40.4 us (16%)
  other arithmetic  14.7 us (6%)
  between operations  4.65 us (2%)
    ppermute x38, starting transfers between devices, send(): return lax.ppermute(x, AXES, route(**to))  51.8 us
    ppermute x38, waiting for transfers between devices, send(): return lax.ppermute(x, AXES, route(**to))  41.4 us
    pallas_call x4, Pallas kernels, score(): pl.pallas_call(functools.partial(score_kernel, rows, prev is None, scale)...  40.6 us
    unnamed x87, local copies, waits for them, and re-layouts  31.8 us
    pallas_call x4, Pallas kernels, query_part(): pl.pallas_call(functools.partial(query_kernel, groups), out_shape=jax.Sha...  27.3 us
    pallas_call x4, Pallas kernels, passage_part(): pl.pallas_call(functools.partial(passage_kernel, tuple(rows), scale), out...  22.2 us
  transfers between devices with their start and end apart: 38, of which 9 were waited for; matrix products, arithmetic and copies ran while one was open for 9% of the time, Pallas kernels for 36%

profile of v1, /device:TPU:0, one launch (start us, length us, event | category | flops | bytes accessed | tf_op | source)
XLA Modules:
  0.0 247.8 jit_solution(6205666725337766463)
XLA Ops:
  7.4 7.8 %collective-permute-done.refs_0_ = f32[128,1024]{1,0:T(8,128)S(1)} collective-permute-done((f32[128,1024]{1,0:T(8,128)}, f32[128,1024]{1,0:T(8,128)S(1)}, u32[]{:S(2)}, u32[]{:S(2)}) %collective-permute-start) | collective-permute-done | bytes 524320 | tf_op jit(solution)/shard_map/ppermute | solution.py:31
  19.8 3.3 %collective-permute-start.10 = (f32[64,1024]{1,0:T(8,128)S(1)}, f32[64,1024]{1,0:T(8,128)S(1)}, u32[]{:S(2)}, u32[]{:S(2)}) collective-permute-start(f32[64,1024]{1,0:T(8,128)S(1)} %slice.232), channel_id=1, source_target_pairs={{0,96},{1,97},{2,98},{3,99},{4,100},{5,101},{6,102},{7,103},{8,104... | collective-permute-start | bytes 786440 | tf_op jit(solution)/shard_map/ppermute | solution.py:31
  23.1 9.1 %collective-permute-done.1.refs_0_ = f32[128,1024]{1,0:T(8,128)S(1)} collective-permute-done((f32[128,1024]{1,0:T(8,128)S(1)}, f32[128,1024]{1,0:T(8,128)S(1)}, u32[]{:S(2)}, u32[]{:S(2)}) %collective-permute-start.1) | collective-permute-done | bytes 524320 | tf_op jit(solution)/shard_map/ppermute | solution.py:31
  33.0 3.2 %collective-permute-start.4 = (f32[64,1024]{1,0:T(8,128)}, f32[64,1024]{1,0:T(8,128)S(1)}, u32[]{:S(2)}, u32[]{:S(2)}) collective-permute-start(f32[64,1024]{1,0:T(8,128)} %slice.230), channel_id=1, source_target_pairs={{0,96},{1,97},{2,98},{3,99},{4,100},{5,101},{6,102},{7,103},{8,104... | collective-permute-start | bytes 786440 | tf_op jit(solution)/shard_map/ppermute | solution.py:31
  36.3 2.2 copy-done.24
  38.4 4.7 %split_rows.1 = (bf16[2048,1024]{1,0:T(8,128)(2,1)S(1)}, bf16[2048,1024]{1,0:T(8,128)(2,1)S(1)}) custom-call(f32[1024,1024]{1,0:T(8,128)S(1)} %copy-done.24, f32[1024,1024]{1,0:T(8,128)} %collective-permute-done.5.b_ref), custom_call_target="tpu_custom_call" | custom-call | flops 4194304 | bytes 16777216 | tf_op jit(solution)/shard_map/split_rows/pallas_call | solution.py:58
  43.2 5.8 %score_128.2 = (f32[128,2048]{1,0:T(8,128)S(1)}, f32[8,2048]{1,0:T(8,128)S(1)}, bf16[128,1024]{1,0:T(8,128)(2,1)S(1)}, bf16[128,1024]{1,0:T(8,128)(2,1)S(1)}) custom-call(s32[2]{0:T(128)S(1)} %pad_add_fusion.4.base_ref, f32[128,1024]{1,0:T(8,128)S(1)} %copy-done.25, bf16[2048,1024]{1,0:T(8,128)(2,1)S(1)} %get-tuple-element.27.refs_1_.refs_3_.refs_4_.refs_2_.qh_ref, ...), custom_call_target="tpu_custom_call" | custom-call | flops 1610612736 | bytes 9961472 | tf_op jit(solution)/shard_map/score_128/pallas_call | solution.py:156
  49.0 13.9 %score_384.2 = (f32[384,2048]{1,0:T(8,128)S(1)}, f32[8,2048]{1,0:T(8,128)S(1)}, bf16[384,1024]{1,0:T(8,128)(2,1)S(1)}, bf16[384,1024]{1,0:T(8,128)(2,1)S(1)}) custom-call(s32[3]{0:T(128)S(1)} %pad_add_fusion.3.base_ref, f32[128,1024]{1,0:T(8,128)S(1)} %collective-permute-done.refs_0_, f32[128,1024]{1,0:T(8,128)S(1)} %copy-done.36, ...), custom_call_target="tpu_custom_call" | custom-call | flops 4831838208 | bytes 13107200 | tf_op jit(solution)/shard_map/score_384/pallas_call | solution.py:156
  63.0 15.2 %score_384.3 = (f32[384,2048]{1,0:T(8,128)S(1)}, f32[8,2048]{1,0:T(8,128)S(1)}, bf16[384,1024]{1,0:T(8,128)(2,1)S(1)}, bf16[384,1024]{1,0:T(8,128)(2,1)S(1)}) custom-call(s32[4]{0:T(128)S(1)} %pad_add_fusion.2.base_ref, f32[128,1024]{1,0:T(8,128)S(1)} %collective-permute-done.1.refs_0_, f32[128,1024]{1,0:T(8,128)S(1)} %collective-permute-done.3.refs_1_, ...), custom_call_target="tpu_custom_call" | custom-call | flops 4831838208 | bytes 13107200 | tf_op jit(solution)/shard_map/score_384/pallas_call | solution.py:156
  82.6 5.6 %score_128.3 = (f32[128,2048]{1,0:T(8,128)S(1)}, f32[8,2048]{1,0:T(8,128)S(1)}, bf16[128,1024]{1,0:T(8,128)(2,1)S(1)}, bf16[128,1024]{1,0:T(8,128)(2,1)S(1)}) custom-call(s32[2]{0:T(128)S(1)} %pad_add_fusion.1.base_ref, f32[64,1024]{1,0:T(8,128)S(1)} %collective-permute-done.2.refs_0_, f32[64,1024]{1,0:T(8,128)S(1)} %copy-done.34, ...), custom_call_target="tpu_custom_call" | custom-call | flops 1610612736 | bytes 9961472 | tf_op jit(solution)/shard_map/score_128/pallas_call | solution.py:156
  89.8 6.3 %query_part.4 = f32[512,1024]{1,0:T(8,128)S(1)} custom-call(f32[128,2048]{1,0:T(8,128)S(1)} %get-tuple-element.33.refs_0_.e_ref, f32[384,2048]{1,0:T(8,128)S(1)} %get-tuple-element.34.refs_1_.e_ref, f32[384,2048]{1,0:T(8,128)} %copy-done.14, f32[128,2048]{1,0:T(8,128)S(1)} %get-tuple-element.36.refs_3_.e_ref, ...), custom_call_target="tpu_custom_call" | custom-call | flops 3221225472 | bytes 8388608 | tf_op jit(solution)/shard_map/query_part/pallas_call | solution.py:211
  99.2 6.3 %query_part.5 = f32[512,1024]{1,0:T(8,128)S(1)} custom-call(f32[128,2048]{1,0:T(8,128)S(1)} %get-tuple-element.33.refs_0_.e_ref, f32[384,2048]{1,0:T(8,128)S(1)} %get-tuple-element.34.refs_1_.e_ref, f32[384,2048]{1,0:T(8,128)} %copy-done.14, f32[128,2048]{1,0:T(8,128)S(1)} %get-tuple-element.36.refs_3_.e_ref, ...), custom_call_target="tpu_custom_call" | custom-call | flops 3221225472 | bytes 8388608 | tf_op jit(solution)/shard_map/query_part/pallas_call | solution.py:211
  106.9 3.0 %collective-permute-start.13 = (f32[3,2048]{1,0:T(4,128)S(1)}, f32[3,2048]{1,0:T(4,128)S(1)}, u32[]{:S(2)}, u32[]{:S(2)}) collective-permute-start(f32[3,2048]{1,0:T(4,128)S(1)} %pad_maximum_fusion.9), channel_id=1, source_target_pairs={{0,4},{1,5},{2,6},{3,7},{4,0},{5,1},{6,2},{7,3},{8,12},{9,13},{10,... | collective-permute-start | bytes 73736 | tf_op jit(solution)/shard_map/ppermute | solution.py:31
  109.9 7.3 %query_part.6 = f32[512,1024]{1,0:T(8,128)} custom-call(f32[128,2048]{1,0:T(8,128)S(1)} %get-tuple-element.33.refs_0_.e_ref, f32[384,2048]{1,0:T(8,128)S(1)} %get-tuple-element.34.refs_1_.e_ref, f32[384,2048]{1,0:T(8,128)} %copy-done.14, f32[128,2048]{1,0:T(8,128)S(1)} %get-tuple-element.36.refs_3_.e_ref, ...), custom_call_target="tpu_custom_call" | custom-call | flops 3221225472 | bytes 8388608 | tf_op jit(solution)/shard_map/query_part/pallas_call | solution.py:211
  117.3 3.1 %collective-permute-start.14 = (f32[3,2048]{1,0:T(4,128)S(1)}, f32[3,2048]{1,0:T(4,128)}, u32[]{:S(2)}, u32[]{:S(2)}) collective-permute-start(f32[3,2048]{1,0:T(4,128)S(1)} %pad_maximum_fusion.10), channel_id=1, source_target_pairs={{0,1},{1,0},{2,3},{3,2},{4,5},{5,4},{6,7},{7,6},{8,9},{9,8},{10,11... | collective-permute-start | bytes 73736 | tf_op jit(solution)/shard_map/ppermute | solution.py:31
  120.4 7.3 %query_part.7 = f32[512,1024]{1,0:T(8,128)} custom-call(f32[128,2048]{1,0:T(8,128)S(1)} %get-tuple-element.33.refs_0_.e_ref, f32[384,2048]{1,0:T(8,128)S(1)} %get-tuple-element.34.refs_1_.e_ref, f32[384,2048]{1,0:T(8,128)} %copy-done.14, f32[128,2048]{1,0:T(8,128)S(1)} %get-tuple-element.36.refs_3_.e_ref, ...), custom_call_target="tpu_custom_call" | custom-call | flops 3221225472 | bytes 8388608 | tf_op jit(solution)/shard_map/query_part/pallas_call | solution.py:211
  130.0 2.8 %fusion.36 = (f32[1,2048]{1,0:T(1,128)S(1)}, f32[1,2048]{1,0:T(1,128)S(1)}, f32[1,2048]{1,0:T(1,128)S(1)}, f32[2048]{0:T(1024)}, f32[1,2048]{1,0:T(1,128)}) fusion(f32[1,2048]{1,0:T(1,128)S(1)} %get-tuple-element.89, f32[1,2048]{1,0:T(1,128)S(1)} %get-tuple-element.90, f32[3,2048]{1,0:T(4,128)} %collective-permute-done.14, f32[]{:T(128)} %broadcast.62, ...), kind=kLoop, calls=%fused_computation.104 | loop fusion | flops 22528 | bytes 90116 | tf_op jit(solution)/shard_map/add | solution.py:350
  132.7 2.2 copy-done.1
  134.9 2.2 copy-done.6
  138.3 3.7 %passage_part_128.2 = f32[128,1024]{1,0:T(8,128)S(1)} custom-call(f32[128,2048]{1,0:T(8,128)S(1)} %copy-done.17, f32[8,2048]{1,0:T(8,128)S(1)} %get-tuple-element.32.refs_7_.stat_ref, f32[8,2048]{1,0:T(8,128)S(1)} %broadcast_in_dim.8.lse_ref, bf16[2048,1024]{1,0:T(8,128)(2,1)S(1)} %copy-done.1, bf16[2048,1024]{1,0:T(8,128)(2,1)S(1)} %copy-done.6), custom_call_target="tpu_custom_call" | custom-call | flops 1610612736 | bytes 9961472 | tf_op jit(solution)/shard_map/passage_part_128/pallas_call | solution.py:250
  142.9 7.4 %passage_part_384.3 = (f32[128,1024]{1,0:T(8,128)S(1)}, f32[128,1024]{1,0:T(8,128)S(1)}, f32[128,1024]{1,0:T(8,128)S(1)}) custom-call(f32[384,2048]{1,0:T(8,128)S(1)} %copy-done.15, f32[8,2048]{1,0:T(8,128)S(1)} %get-tuple-element.31.refs_5_.refs_6_.stat_ref, f32[8,2048]{1,0:T(8,128)S(1)} %broadcast_in_dim.8.lse_ref, bf16[2048,1024]{1,0:T(8,128)(2,1)S(1)} %copy-done.1, ...), custom_call_target="tpu_custom_call" | custom-call | flops 4831838208 | bytes 13107200 | tf_op jit(solution)/shard_map/passage_part_384/pallas_call | solution.py:250
  163.8 2.2 copy-done.7
  167.9 7.4 %passage_part_384.2 = (f32[128,1024]{1,0:T(8,128)S(1)}, f32[128,1024]{1,0:T(8,128)S(1)}, f32[128,1024]{1,0:T(8,128)S(1)}) custom-call(f32[384,2048]{1,0:T(8,128)S(1)} %copy-done.13, f32[8,2048]{1,0:T(8,128)S(1)} %get-tuple-element.30.refs_7_.refs_5_.stat_ref, f32[8,2048]{1,0:T(8,128)S(1)} %broadcast_in_dim.8.lse_ref, bf16[2048,1024]{1,0:T(8,128)(2,1)S(1)} %copy-done.2, ...), custom_call_target="tpu_custom_call" | custom-call | flops 4831838208 | bytes 13107200 | tf_op jit(solution)/shard_map/passage_part_384/pallas_call | solution.py:250
  176.7 3.9 %collective-permute-done.16 = f32[8,128]{1,0:T(8,128)S(1)} collective-permute-done((f32[8,128]{1,0:T(8,128)S(1)}, f32[8,128]{1,0:T(8,128)S(1)}, u32[]{:S(2)}, u32[]{:S(2)}) %collective-permute-start.16) | collective-permute-done | bytes 4128 | tf_op jit(solution)/shard_map/ppermute | solution.py:31
  181.4 2.4 collective-permute-start.36
  191.3 4.1 %collective-permute-done.22 = f32[64,1024]{1,0:T(8,128)S(1)} collective-permute-done((f32[64,1024]{1,0:T(8,128)S(1)}, f32[64,1024]{1,0:T(8,128)S(1)}, u32[]{:S(2)}, u32[]{:S(2)}) %collective-permute-start.22) | collective-permute-done | bytes 262176 | tf_op jit(solution)/shard_map/ppermute | solution.py:31
  200.8 6.5 %collective-permute-done.23 = f32[128,1024]{1,0:T(8,128)S(1)} collective-permute-done((f32[128,1024]{1,0:T(8,128)S(1)}, f32[128,1024]{1,0:T(8,128)S(1)}, u32[]{:S(2)}, u32[]{:S(2)}) %collective-permute-start.23) | collective-permute-done | bytes 524320 | tf_op jit(solution)/shard_map/ppermute | solution.py:31
  207.3 2.7 %collective-permute-start.37 = (f32[128,1024]{1,0:T(8,128)S(1)}, f32[128,1024]{1,0:T(8,128)}, u32[]{:S(2)}, u32[]{:S(2)}) collective-permute-start(f32[128,1024]{1,0:T(8,128)S(1)} %pad_maximum_fusion.7), channel_id=1, source_target_pairs={{0,96},{1,97},{2,98},{3,99},{4,100},{5,101},{6,102},{7,103},{8,104... | collective-permute-start | bytes 1572872 | tf_op jit(solution)/shard_map/ppermute | solution.py:31
  219.4 5.9 %collective-permute-done.25 = f32[64,1024]{1,0:T(8,128)S(1)} collective-permute-done((f32[64,1024]{1,0:T(8,128)S(1)}, f32[64,1024]{1,0:T(8,128)S(1)}, u32[]{:S(2)}, u32[]{:S(2)}) %collective-permute-start.25) | collective-permute-done | bytes 262176 | tf_op jit(solution)/shard_map/ppermute | solution.py:31
  228.2 4.3 %collective-permute-start.28 = (f32[128,1024]{1,0:T(8,128)}, f32[128,1024]{1,0:T(8,128)}, u32[]{:S(2)}, u32[]{:S(2)}) collective-permute-start(f32[128,1024]{1,0:T(8,128)} %pad_maximum_fusion.3), channel_id=1, source_target_pairs={{0,6},{1,7},{2,0},{3,1},{4,2},{5,3},{6,4},{7,5},{8,14},{9,15},{10,... | collective-permute-start | bytes 1572872 | tf_op jit(solution)/shard_map/ppermute | solution.py:31
  236.9 3.7 %passage_part_128.3 = f32[128,1024]{1,0:T(8,128)S(1)} custom-call(f32[128,2048]{1,0:T(8,128)S(1)} %get-tuple-element.33.refs_0_.e_ref, f32[8,2048]{1,0:T(8,128)S(1)} %get-tuple-element.29.refs_6_.refs_4_.stat_ref, f32[8,2048]{1,0:T(8,128)S(1)} %broadcast_in_dim.8.lse_ref, bf16[2048,1024]{1,0:T(8,128)(2,1)S(1)} %copy-done.3, bf16[2048,1024]{1,0:T(8,128)(2,1)S(1)} %copy-done.8), custom_call_target="tpu_custom_call" | custom-call | flops 1610612736 | bytes 9961472 | tf_op jit(solution)/shard_map/passage_part_128/pallas_call | solution.py:250
  243.2 3.5 %multiply_add_fusion = (f32[128,1024]{1,0:T(8,128)}, f32[128,1024]{1,0:T(8,128)}) fusion(f32[1024,1024]{1,0:T(8,128)} %a_ref.1, s32[]{:T(128)S(6)} %select_n.301, f32[128,1024]{1,0:T(8,128)} %collective-permute-done.33, f32[128,1024]{1,0:T(8,128)} %collective-permute-done.37, f32[128,1024]{1,0:T(8,128)S(1)} %passage_part_128.3, ...), kind=kLoop, calls=%fused_computation.54 | loop fusion | flops 1835008 | bytes 10487304 | tf_op jit(solution)/shard_map/add | solution.py:391
  (209 shorter events, 74.1 us)
Async XLA Ops:
  0.6 35.6 %collective-permute-start.5 = (f32[1024,1024]{1,0:T(8,128)}, f32[1024,1024]{1,0:T(8,128)}, u32[]{:S(2)}, u32[]{:S(2)}) collective-permute-start(f32[1024,1024]{1,0:T(8,128)} %a_ref.1), channel_id=1, source_target_pairs={{0,8},{1,9},{2,10},{3,11},{4,12},{5,13},{6,14},{7,15},{8,0},{9,1},... | collective-permute-start | bytes 12582920 | tf_op jit(solution)/shard_map/ppermute | solution.py:31
  0.7 14.5 %collective-permute-start = (f32[128,1024]{1,0:T(8,128)}, f32[128,1024]{1,0:T(8,128)S(1)}, u32[]{:S(2)}, u32[]{:S(2)}) collective-permute-start(f32[128,1024]{1,0:T(8,128)} %refs_0_.1), channel_id=1, source_target_pairs={{0,16},{1,17},{2,18},{3,19},{4,20},{5,21},{6,22},{7,23},{8,24},{9,... | collective-permute-start | bytes 1572872 | tf_op jit(solution)/shard_map/ppermute | solution.py:31
  2.4 17.2 %collective-permute-start.7 = (f32[128,1024]{1,0:T(8,128)}, f32[128,1024]{1,0:T(8,128)S(1)}, u32[]{:S(2)}, u32[]{:S(2)}) collective-permute-start(f32[128,1024]{1,0:T(8,128)} %refs_0_.1), channel_id=1, source_target_pairs={{0,32},{1,33},{2,34},{3,35},{4,36},{5,37},{6,38},{7,39},{8,40},{9,... | collective-permute-start | bytes 1572872 | tf_op jit(solution)/shard_map/ppermute | solution.py:31
  4.3 15.5 %collective-permute-start.9 = (f32[128,1024]{1,0:T(8,128)}, f32[128,1024]{1,0:T(8,128)S(1)}, u32[]{:S(2)}, u32[]{:S(2)}) collective-permute-start(f32[128,1024]{1,0:T(8,128)} %refs_0_.1), channel_id=1, source_target_pairs={{0,96},{1,97},{2,98},{3,99},{4,100},{5,101},{6,102},{7,103},{8,104... | collective-permute-start | bytes 1572872 | tf_op jit(solution)/shard_map/ppermute | solution.py:31
  7.2 10.1 %collective-permute-start.6 = (s32[8,1024]{1,0:T(8,128)S(1)}, s32[8,1024]{1,0:T(8,128)S(1)}, u32[]{:S(2)}, u32[]{:S(2)}) collective-permute-start(s32[8,1024]{1,0:T(8,128)S(1)} %concatenate.39), channel_id=1, source_target_pairs={{0,8},{1,9},{2,10},{3,11},{4,12},{5,13},{6,14},{7,15},{8,0},{9,1},... | collective-permute-start | bytes 98312 | tf_op jit(solution)/shard_map/ppermute | solution.py:31
  15.3 16.9 %collective-permute-start.1 = (f32[128,1024]{1,0:T(8,128)S(1)}, f32[128,1024]{1,0:T(8,128)S(1)}, u32[]{:S(2)}, u32[]{:S(2)}) collective-permute-start(f32[128,1024]{1,0:T(8,128)S(1)} %collective-permute-done.refs_0_), channel_id=1, source_target_pairs={{0,32},{1,33},{2,34},{3,35},{4,36},{5,37},{6,38},{7,39},{8,40},{9,... | collective-permute-start | bytes 1572872 | tf_op jit(solution)/shard_map/ppermute | solution.py:31
  17.3 15.0 %collective-permute-start.3 = (f32[128,1024]{1,0:T(8,128)S(1)}, f32[128,1024]{1,0:T(8,128)S(1)}, u32[]{:S(2)}, u32[]{:S(2)}) collective-permute-start(f32[128,1024]{1,0:T(8,128)S(1)} %collective-permute-done.refs_0_), channel_id=1, source_target_pairs={{0,96},{1,97},{2,98},{3,99},{4,100},{5,101},{6,102},{7,103},{8,104... | collective-permute-start | bytes 1572872 | tf_op jit(solution)/shard_map/ppermute | solution.py:31
  19.7 43.3 %collective-permute-start.8 = (f32[64,1024]{1,0:T(8,128)S(1)}, f32[64,1024]{1,0:T(8,128)S(1)}, u32[]{:S(2)}, u32[]{:S(2)}) collective-permute-start(f32[64,1024]{1,0:T(8,128)S(1)} %slice.231), channel_id=1, source_target_pairs={{0,32},{1,33},{2,34},{3,35},{4,36},{5,37},{6,38},{7,39},{8,40},{9,... | collective-permute-start | bytes 786440 | tf_op jit(solution)/shard_map/ppermute | solution.py:31
  19.8 43.2 %collective-permute-start.10 = (f32[64,1024]{1,0:T(8,128)S(1)}, f32[64,1024]{1,0:T(8,128)S(1)}, u32[]{:S(2)}, u32[]{:S(2)}) collective-permute-start(f32[64,1024]{1,0:T(8,128)S(1)} %slice.232), channel_id=1, source_target_pairs={{0,96},{1,97},{2,98},{3,99},{4,100},{5,101},{6,102},{7,103},{8,104... | collective-permute-start | bytes 786440 | tf_op jit(solution)/shard_map/ppermute | solution.py:31
  32.2 48.7 %collective-permute-start.2 = (f32[64,1024]{1,0:T(8,128)S(1)}, f32[64,1024]{1,0:T(8,128)S(1)}, u32[]{:S(2)}, u32[]{:S(2)}) collective-permute-start(f32[64,1024]{1,0:T(8,128)S(1)} %slice.229), channel_id=1, source_target_pairs={{0,32},{1,33},{2,34},{3,35},{4,36},{5,37},{6,38},{7,39},{8,40},{9,... | collective-permute-start | bytes 786440 | tf_op jit(solution)/shard_map/ppermute | solution.py:31
  33.0 47.8 %collective-permute-start.4 = (f32[64,1024]{1,0:T(8,128)}, f32[64,1024]{1,0:T(8,128)S(1)}, u32[]{:S(2)}, u32[]{:S(2)}) collective-permute-start(f32[64,1024]{1,0:T(8,128)} %slice.230), channel_id=1, source_target_pairs={{0,96},{1,97},{2,98},{3,99},{4,100},{5,101},{6,102},{7,103},{8,104... | collective-permute-start | bytes 786440 | tf_op jit(solution)/shard_map/ppermute | solution.py:31
  96.2 10.6 %collective-permute-start.12 = (f32[3,2048]{1,0:T(4,128)S(1)}, f32[3,2048]{1,0:T(4,128)S(1)}, u32[]{:S(2)}, u32[]{:S(2)}) collective-permute-start(f32[3,2048]{1,0:T(4,128)S(1)} %pad_maximum_fusion.8), channel_id=1, source_target_pairs={{0,2},{1,3},{2,0},{3,1},{4,6},{5,7},{6,4},{7,5},{8,10},{9,11},{10,... | collective-permute-start | bytes 73736 | tf_op jit(solution)/shard_map/ppermute | solution.py:31
  106.9 10.3 %collective-permute-start.13 = (f32[3,2048]{1,0:T(4,128)S(1)}, f32[3,2048]{1,0:T(4,128)S(1)}, u32[]{:S(2)}, u32[]{:S(2)}) collective-permute-start(f32[3,2048]{1,0:T(4,128)S(1)} %pad_maximum_fusion.9), channel_id=1, source_target_pairs={{0,4},{1,5},{2,6},{3,7},{4,0},{5,1},{6,2},{7,3},{8,12},{9,13},{10,... | collective-permute-start | bytes 73736 | tf_op jit(solution)/shard_map/ppermute | solution.py:31
  117.3 12.2 %collective-permute-start.14 = (f32[3,2048]{1,0:T(4,128)S(1)}, f32[3,2048]{1,0:T(4,128)}, u32[]{:S(2)}, u32[]{:S(2)}) collective-permute-start(f32[3,2048]{1,0:T(4,128)S(1)} %pad_maximum_fusion.10), channel_id=1, source_target_pairs={{0,1},{1,0},{2,3},{3,2},{4,5},{5,4},{6,7},{7,6},{8,9},{9,8},{10,11... | collective-permute-start | bytes 73736 | tf_op jit(solution)/shard_map/ppermute | solution.py:31
  128.3 56.3 %collective-permute-start.18 = (f32[512,1024]{1,0:T(8,128)}, f32[512,1024]{1,0:T(8,128)}, u32[]{:S(2)}, u32[]{:S(2)}) collective-permute-start(f32[512,1024]{1,0:T(8,128)} %query_part.6), channel_id=1, source_target_pairs={{0,8},{1,9},{2,10},{3,11},{4,12},{5,13},{6,14},{7,15},{8,0},{9,1},... | collective-permute-start | bytes 6291464 | tf_op jit(solution)/shard_map/ppermute | solution.py:31
  128.3 58.2 %collective-permute-start.19 = (f32[512,1024]{1,0:T(8,128)}, f32[512,1024]{1,0:T(8,128)}, u32[]{:S(2)}, u32[]{:S(2)}) collective-permute-start(f32[512,1024]{1,0:T(8,128)} %query_part.7), channel_id=1, source_target_pairs={{0,8},{1,9},{2,10},{3,11},{4,12},{5,13},{6,14},{7,15},{8,0},{9,1},... | collective-permute-start | bytes 6291464 | tf_op jit(solution)/shard_map/ppermute | solution.py:31
  156.1 19.3 %collective-permute-start.15 = (f32[8,128]{1,0:T(8,128)S(1)}, f32[8,128]{1,0:T(8,128)S(1)}, u32[]{:S(2)}, u32[]{:S(2)}) collective-permute-start(f32[8,128]{1,0:T(8,128)S(1)} %broadcast_in_dim.6), channel_id=1, source_target_pairs={{0,32},{1,33},{2,34},{3,35},{4,36},{5,37},{6,38},{7,39},{8,40},{9,... | collective-permute-start | bytes 12296 | tf_op jit(solution)/shard_map/ppermute | solution.py:31
  157.3 24.1 %collective-permute-start.29 = (f32[64,1024]{1,0:T(8,128)S(1)}, f32[64,1024]{1,0:T(8,128)S(1)}, u32[]{:S(2)}, u32[]{:S(2)}) collective-permute-start(f32[64,1024]{1,0:T(8,128)S(1)} %get-tuple-element.70), channel_id=1, source_target_pairs={{0,32},{1,33},{2,34},{3,35},{4,36},{5,37},{6,38},{7,39},{8,40},{9,... | collective-permute-start | bytes 786440 | tf_op jit(solution)/shard_map/ppermute | solution.py:31
  159.3 24.5 %collective-permute-start.31 = (f32[64,1024]{1,0:T(8,128)S(1)}, f32[64,1024]{1,0:T(8,128)S(1)}, u32[]{:S(2)}, u32[]{:S(2)}) collective-permute-start(f32[64,1024]{1,0:T(8,128)S(1)} %get-tuple-element.71), channel_id=1, source_target_pairs={{0,96},{1,97},{2,98},{3,99},{4,100},{5,101},{6,102},{7,103},{8,104... | collective-permute-start | bytes 786440 | tf_op jit(solution)/shard_map/ppermute | solution.py:31
  180.6 17.1 %collective-permute-start.34 = (f32[64,1024]{1,0:T(8,128)S(1)}, f32[64,1024]{1,0:T(8,128)S(1)}, u32[]{:S(2)}, u32[]{:S(2)}) collective-permute-start(f32[64,1024]{1,0:T(8,128)S(1)} %get-tuple-element.64), channel_id=1, source_target_pairs={{0,32},{1,33},{2,34},{3,35},{4,36},{5,37},{6,38},{7,39},{8,40},{9,... | collective-permute-start | bytes 786440 | tf_op jit(solution)/shard_map/ppermute | solution.py:31
  181.4 17.8 %collective-permute-start.36 = (f32[64,1024]{1,0:T(8,128)S(1)}, f32[64,1024]{1,0:T(8,128)S(1)}, u32[]{:S(2)}, u32[]{:S(2)}) collective-permute-start(f32[64,1024]{1,0:T(8,128)S(1)} %get-tuple-element.65), channel_id=1, source_target_pairs={{0,96},{1,97},{2,98},{3,99},{4,100},{5,101},{6,102},{7,103},{8,104... | collective-permute-start | bytes 786440 | tf_op jit(solution)/shard_map/ppermute | solution.py:31
  183.8 44.4 %collective-permute-start.17 = (f32[8,128]{1,0:T(8,128)S(1)}, f32[8,128]{1,0:T(8,128)S(1)}, u32[]{:S(2)}, u32[]{:S(2)}) collective-permute-start(f32[8,128]{1,0:T(8,128)S(1)} %fusion.50), channel_id=1, source_target_pairs={{0,16},{1,17},{2,18},{3,19},{4,20},{5,21},{6,22},{7,23},{8,24},{9,... | collective-permute-start | bytes 12296 | tf_op jit(solution)/shard_map/ppermute | solution.py:31
  195.4 15.9 %collective-permute-start.32 = (f32[128,1024]{1,0:T(8,128)S(1)}, f32[128,1024]{1,0:T(8,128)S(1)}, u32[]{:S(2)}, u32[]{:S(2)}) collective-permute-start(f32[128,1024]{1,0:T(8,128)S(1)} %pad_maximum_fusion.5), channel_id=1, source_target_pairs={{0,96},{1,97},{2,98},{3,99},{4,100},{5,101},{6,102},{7,103},{8,104... | collective-permute-start | bytes 1572872 | tf_op jit(solution)/shard_map/ppermute | solution.py:31
  196.9 16.5 %collective-permute-start.30 = (f32[128,1024]{1,0:T(8,128)S(1)}, f32[128,1024]{1,0:T(8,128)S(1)}, u32[]{:S(2)}, u32[]{:S(2)}) collective-permute-start(f32[128,1024]{1,0:T(8,128)S(1)} %pad_maximum_fusion.4), channel_id=1, source_target_pairs={{0,32},{1,33},{2,34},{3,35},{4,36},{5,37},{6,38},{7,39},{8,40},{9,... | collective-permute-start | bytes 1572872 | tf_op jit(solution)/shard_map/ppermute | solution.py:31
  197.7 9.6 %collective-permute-start.23 = (f32[128,1024]{1,0:T(8,128)S(1)}, f32[128,1024]{1,0:T(8,128)S(1)}, u32[]{:S(2)}, u32[]{:S(2)}) collective-permute-start(f32[128,1024]{1,0:T(8,128)S(1)} %pad_maximum_fusion.1), channel_id=1, source_target_pairs={{0,6},{1,7},{2,0},{3,1},{4,2},{5,3},{6,4},{7,5},{8,14},{9,15},{10,... | collective-permute-start | bytes 1572872 | tf_op jit(solution)/shard_map/ppermute | solution.py:31
  199.2 10.9 %collective-permute-start.21 = (f32[128,1024]{1,0:T(8,128)S(1)}, f32[128,1024]{1,0:T(8,128)S(1)}, u32[]{:S(2)}, u32[]{:S(2)}) collective-permute-start(f32[128,1024]{1,0:T(8,128)S(1)} %pad_maximum_fusion), channel_id=1, source_target_pairs={{0,2},{1,3},{2,4},{3,5},{4,6},{5,7},{6,0},{7,1},{8,10},{9,11},{10,... | collective-permute-start | bytes 1572872 | tf_op jit(solution)/shard_map/ppermute | solution.py:31
  207.3 25.1 %collective-permute-start.37 = (f32[128,1024]{1,0:T(8,128)S(1)}, f32[128,1024]{1,0:T(8,128)}, u32[]{:S(2)}, u32[]{:S(2)}) collective-permute-start(f32[128,1024]{1,0:T(8,128)S(1)} %pad_maximum_fusion.7), channel_id=1, source_target_pairs={{0,96},{1,97},{2,98},{3,99},{4,100},{5,101},{6,102},{7,103},{8,104... | collective-permute-start | bytes 1572872 | tf_op jit(solution)/shard_map/ppermute | solution.py:31
  210.0 32.4 %collective-permute-start.35 = (f32[128,1024]{1,0:T(8,128)}, f32[128,1024]{1,0:T(8,128)}, u32[]{:S(2)}, u32[]{:S(2)}) collective-permute-start(f32[128,1024]{1,0:T(8,128)} %pad_maximum_fusion.6), channel_id=1, source_target_pairs={{0,32},{1,33},{2,34},{3,35},{4,36},{5,37},{6,38},{7,39},{8,40},{9,... | collective-permute-start | bytes 1572872 | tf_op jit(solution)/shard_map/ppermute | solution.py:31
  214.3 28.2 %collective-permute-start.33 = (f32[128,1024]{1,0:T(8,128)}, f32[128,1024]{1,0:T(8,128)}, u32[]{:S(2)}, u32[]{:S(2)}) collective-permute-start(f32[128,1024]{1,0:T(8,128)} %add_add_fusion), channel_id=1, source_target_pairs={{0,16},{1,17},{2,18},{3,19},{4,20},{5,21},{6,22},{7,23},{8,24},{9,... | collective-permute-start | bytes 1572872 | tf_op jit(solution)/shard_map/ppermute | solution.py:31
  225.3 17.2 %collective-permute-start.24 = (f32[128,1024]{1,0:T(8,128)}, f32[128,1024]{1,0:T(8,128)}, u32[]{:S(2)}, u32[]{:S(2)}) collective-permute-start(f32[128,1024]{1,0:T(8,128)} %get-tuple-element.57), channel_id=1, source_target_pairs={{0,1},{1,0},{2,3},{3,2},{4,5},{5,4},{6,7},{7,6},{8,9},{9,8},{10,11... | collective-permute-start | bytes 1572872 | tf_op jit(solution)/shard_map/ppermute | solution.py:31
  228.2 14.3 %collective-permute-start.28 = (f32[128,1024]{1,0:T(8,128)}, f32[128,1024]{1,0:T(8,128)}, u32[]{:S(2)}, u32[]{:S(2)}) collective-permute-start(f32[128,1024]{1,0:T(8,128)} %pad_maximum_fusion.3), channel_id=1, source_target_pairs={{0,6},{1,7},{2,0},{3,1},{4,2},{5,3},{6,4},{7,5},{8,14},{9,15},{10,... | collective-permute-start | bytes 1572872 | tf_op jit(solution)/shard_map/ppermute | solution.py:31
  232.5 10.7 %collective-permute-start.26 = (f32[128,1024]{1,0:T(8,128)}, f32[128,1024]{1,0:T(8,128)}, u32[]{:S(2)}, u32[]{:S(2)}) collective-permute-start(f32[128,1024]{1,0:T(8,128)} %pad_maximum_fusion.2), channel_id=1, source_target_pairs={{0,2},{1,3},{2,4},{3,5},{4,6},{5,7},{6,0},{7,1},{8,10},{9,11},{10,... | collective-permute-start | bytes 1572872 | tf_op jit(solution)/shard_map/ppermute | solution.py:31
  (49 other events, 431.7 us)
